TPU v7x, 256 devices: a whole 4x4x8 slice. The times are simulated.
256 devices in a mesh: coil: 8 (over z_hi, x), ro: 32 (over y, z_lo, core).
Axes of the slice: x: 4, y: 4, z: 8 (z_hi: 2, z_lo: 4; z = z_hi * 4 + z_lo), core: 2. Of those that a mesh axis runs over, the one named last changes fastest.
Arguments:
- kspace: bfloat16 [2, 64, 32, 448, 320], P(None, 'coil', None, 'ro'), may hold values from -884272563206990856199 to 884272563206990856199
- sensitivity: bfloat16 [2, 64, 32, 448, 320], P(None, 'coil', 'ro'), may hold values from -0.75 to 0.75
- sampled: int32 [32, 448], replicated, may hold values 0 or 1
- pole_y: int32 [32, 320], replicated, may hold values from 4 to 112
- order_y: int32 [32, 320], replicated, may hold values from 1 to 3
- pole_z: int32 [32, 448], replicated, may hold values from 4 to 80
- order_z: int32 [32, 448], replicated, may hold values from 1 to 3
Outputs:
- image: float32 [2, 32, 448, 320], P(None, 'ro', 'coil')
All inputs are finite; a program needn't handle non-finite values.
Results may differ from a plain program's by a relative error of at most 0.0056.
Values may be sent and summed in bfloat16 or wider, within the bound.
A program may use at most 128 MiB of HBM per device.

v0:
```python
import math
import jax
import jax.numpy as jnp
from jax import lax
from jax.sharding import PartitionSpec as P


def dft_tables(length):
    index = jnp.arange(length, dtype=jnp.int32)
    product = index[:, None] * index[None, :] % length
    angle = product.astype(jnp.float32) * (2.0 * math.pi / length)
    factor = 1.0 / math.sqrt(length)
    return (
        (jnp.cos(angle) * factor).astype(jnp.bfloat16),
        (jnp.sin(angle) * factor).astype(jnp.bfloat16),
    )


def line_window(frequency, pole, degree):
    quotient = frequency / pole.astype(jnp.float32)
    return 1.0 / (1.0 + jnp.power(quotient, 2.0 * degree.astype(jnp.float32)))


def kz_transform(filtered, kz_cosine, kz_sine):
    real_part, imag_part = (filtered[0], filtered[1])
    hyb_real = jnp.einsum(
        "cakz,zn->cakn", real_part, kz_cosine, preferred_element_type=jnp.float32
    ) - jnp.einsum("cakz,zn->cakn", imag_part, kz_sine, preferred_element_type=jnp.float32)
    hyb_imag = jnp.einsum(
        "cakz,zn->cakn", real_part, kz_sine, preferred_element_type=jnp.float32
    ) + jnp.einsum("cakz,zn->cakn", imag_part, kz_cosine, preferred_element_type=jnp.float32)
    return jnp.stack([hyb_real, hyb_imag]).astype(jnp.bfloat16)


def on_device(kspace, sensitivity, sampled, pole_y, order_y, pole_z, order_z):
    lines_local = kspace.shape[3]
    kz_count = kspace.shape[4]
    ky_count = lines_local * lax.axis_size("ro")
    first_line = lax.axis_index("ro") * lines_local
    kz_cosine, kz_sine = dft_tables(kz_count)
    ky_cosine, ky_sine = dft_tables(ky_count)
    line_index = first_line + jnp.arange(lines_local, dtype=jnp.int32)
    freq_y = jnp.minimum(line_index, ky_count - line_index).astype(jnp.float32)
    col_index = jnp.arange(kz_count, dtype=jnp.int32)
    freq_z = jnp.minimum(col_index, kz_count - col_index).astype(jnp.float32)
    local_sampled = lax.dynamic_slice_in_dim(sampled, first_line, lines_local, 1)
    local_pole_z = lax.dynamic_slice_in_dim(pole_z, first_line, lines_local, 1)
    local_order_z = lax.dynamic_slice_in_dim(order_z, first_line, lines_local, 1)
    weight_y = local_sampled[:, :, None].astype(jnp.float32) * line_window(
        freq_y[None, :, None], pole_y[:, None, :], order_y[:, None, :]
    )
    weight_z = line_window(
        freq_z[None, None, :], local_pole_z[:, :, None], local_order_z[:, :, None]
    )
    filtered = (kspace.astype(jnp.float32) * (weight_y * weight_z)).astype(jnp.bfloat16)
    hybrid = kz_transform(filtered, kz_cosine, kz_sine)
    moved = lax.all_to_all(hybrid, "ro", split_axis=2, concat_axis=3, tiled=True)
    hyb_real, hyb_imag = (moved[0], moved[1])
    img_real = jnp.einsum(
        "nk,cakz->canz", ky_cosine, hyb_real, preferred_element_type=jnp.float32
    ) - jnp.einsum("nk,cakz->canz", ky_sine, hyb_imag, preferred_element_type=jnp.float32)
    img_imag = jnp.einsum(
        "nk,cakz->canz", ky_sine, hyb_real, preferred_element_type=jnp.float32
    ) + jnp.einsum("nk,cakz->canz", ky_cosine, hyb_imag, preferred_element_type=jnp.float32)
    map_real = sensitivity[0]
    map_imag = sensitivity[1]
    out_real = jnp.sum(map_real * img_real + map_imag * img_imag, axis=0)
    out_imag = jnp.sum(map_real * img_imag - map_imag * img_real, axis=0)
    partial_image = jnp.stack([out_real, out_imag])
    return lax.psum_scatter(partial_image, "coil", scatter_dimension=2, tiled=True)


def solution(mesh):
    return jax.shard_map(
        on_device,
        mesh=mesh,
        in_specs=(
            P(None, "coil", None, "ro", None),
            P(None, "coil", "ro", None, None),
            P(),
            P(),
            P(),
            P(),
            P(),
        ),
        out_specs=P(None, "ro", "coil", None),
        check_vma=False,
    )
```

profile of v0, /device:TPU:8, one launch (start us, length us, event | category | flops | bytes accessed | tf_op | source)
XLA Modules:
  0.0 342.3 jit_solution(6022209747926040694)
XLA Ops:
  6.6 0.9 constant_dynamic-slice_fusion
  7.8 0.8 convert_element_type.114
  8.6 0.8 convert_multiply_fusion.4
  9.4 2.3 fusion.15
  11.7 3.8 %multiply_convert_fusion = bf16[2,8,32,14,320]{4,2,3,1,0:T(8,128)(2,1)S(1)} fusion(bf16[2,8,32,14,320]{4,2,3,1,0:T(8,128)(2,1)} %param.7, f32[32,14,320]{2,0,1:T(8,128)S(1)} %fusion.15), kind=kLoop, calls=%fused_computation | loop fusion | flops 6881280 | bytes 9748480 | tf_op jit(solution)/shard_map/convert_element_type | solution.py:55
  15.5 3.4 fusion.7
  18.9 3.4 fusion.6
  22.3 3.8 %fusion.4 = bf16[1,8,32,14,320]{4,2,3,1,0:T(8,128)(2,1)S(1)} fusion(f32[8,32,14,320]{3,1,2,0:T(8,128)S(1)} %fusion.7, bf16[2,8,32,14,320]{4,2,3,1,0:T(8,128)(2,1)S(1)} %multiply_convert_fusion), kind=kOutput, calls=%fused_computation.12 | convolution fusion | flops 737423360 | bytes 10551296 | tf_op jit(solution)/shard_map/cakz,zn->cakn/dot_general | solution.py:28
  26.1 3.6 %fusion.5 = bf16[1,8,32,14,320]{4,2,3,1,0:T(8,128)(2,1)S(1)} fusion(f32[8,32,14,320]{3,1,2,0:T(8,128)S(1)} %fusion.6, bf16[2,8,32,14,320]{4,2,3,1,0:T(8,128)(2,1)S(1)} %multiply_convert_fusion), kind=kOutput, calls=%fused_computation.13 | convolution fusion | flops 737423360 | bytes 10551296 | tf_op jit(solution)/shard_map/cakz,zn->cakn/dot_general | solution.py:31
  29.7 1.1 pad_maximum_fusion
  30.8 3.3 copy.53
  34.1 130.9 %all_to_all.4 = bf16[2,8,32,14,320]{4,1,3,0,2:T(8,128)(2,1)S(1)} all-to-all(bf16[2,8,32,14,320]{4,1,3,0,2:T(8,128)(2,1)S(1)} %copy.53), channel_id=1, replica_groups=mesh['coil'=8,'ro'=32] {'ro'}, dimensions={2} | all-to-all | bytes 9175040 | tf_op jit(solution)/shard_map/all_to_all | solution.py:57
  165.0 3.1 fusion.72
  168.1 3.7 %copy.54 = bf16[8,448,320]{1,2,0:T(8,128)(2,1)S(1)} copy(bf16[8,448,320]{2,0,1:T(8,128)(2,1)} %bitcast.70) | data formatting | bytes 4587520 | tf_op jit(solution)/shard_map/reshape.4
  171.8 8.5 %fusion.26 = f32[8,320,448]{2,1,0:T(8,128)} fusion(bf16[8,448,320]{1,2,0:T(8,128)(2,1)S(1)} %copy.54), kind=kOutput, calls=%fused_computation.51 | convolution fusion | flops 1029812224 | bytes 6881280 | tf_op jit(solution)/shard_map/nk,cakz->canz/dot_general | solution.py:62
  180.4 8.5 %fusion.30 = f32[8,320,448]{2,1,0:T(8,128)} fusion(bf16[8,448,320]{1,2,0:T(8,128)(2,1)S(1)} %copy.54), kind=kOutput, calls=%fused_computation.52 | convolution fusion | flops 1029812224 | bytes 6881280 | tf_op jit(solution)/shard_map/nk,cakz->canz/dot_general | solution.py:59
  188.9 3.7 %copy.55 = bf16[8,448,320]{1,2,0:T(8,128)(2,1)S(1)} copy(bf16[8,448,320]{2,0,1:T(8,128)(2,1)} %bitcast.69) | data formatting | bytes 4587520 | tf_op jit(solution)/shard_map/reshape.9
  192.6 8.8 %convolution_add_fusion = f32[8,320,448]{2,1,0:T(8,128)S(1)} fusion(f32[8,320,448]{2,1,0:T(8,128)} %fusion.26, bf16[8,448,320]{1,2,0:T(8,128)(2,1)S(1)} %copy.55), kind=kOutput, calls=%fused_computation.20 | convolution fusion | flops 1030959104 | bytes 11468800 | tf_op jit(solution)/shard_map/nk,cakz->canz/dot_general | solution.py:64
  201.5 9.9 %fusion.1 = (f32[448,320]{0,1:T(8,128)S(1)}, f32[448,320]{0,1:T(8,128)S(1)}) fusion(f32[8,320,448]{2,1,0:T(8,128)S(1)} %convolution_add_fusion, bf16[2,8,1,448,320]{3,4,1,2,0:T(8,128)(2,1)} %bitcast.73, f32[8,320,448]{2,1,0:T(8,128)S(1)} %copy-done.2, bf16[8,448,320]{1,2,0:T(8,128)(2,1)S(1)} %copy.55), kind=kOutput, calls=%fused_computation.9 | convolution fusion | flops 1042141184 | bytes 17203200 | tf_op jit(solution)/shard_map/nk,cakz->canz/dot_general | solution.py:61
  211.5 2.2 copy.59
  213.7 0.6 dynamic-slice
  214.9 118.9 %all-reduce.3.cloned.1.call-done = f32[2,1,448,320]{3,0,1,2:T(2,128)} async-done(((f32[2,1,448,320]{3,0,1,2:T(2,128)}), f32[2,1,448,320]{3,0,1,2:T(2,128)}) %all-reduce.3.cloned.1.call-update) | async-done | bytes 1146896
  333.9 1.0 constant_dynamic-slice_fusion.3
  334.8 0.7 copy.60
  (20 shorter events, 0.5 us)
Async XLA Ops:
  6.5 1.1 copy-start
  6.5 327.3 %all-reduce.3.cloned.1.call-start = ((), (), s32[]{:S(2)}) async-start(), calls=%async_computation.1 | async-start | bytes 2752512
  192.6 8.9 %copy-start.2 = (f32[8,320,448]{2,1,0:T(8,128)S(1)}, f32[8,320,448]{2,1,0:T(8,128)}, u32[]{:S(2)}) copy-start(f32[8,320,448]{2,1,0:T(8,128)} %fusion.30) | copy-start | bytes 13762564
  201.5 134.0 %copy-start.1 = (s32[32,448]{1,0:T(8,128)S(1)}, s32[32,448]{1,0:T(8,128)}, u32[]{:S(2)}) copy-start(s32[32,448]{1,0:T(8,128)} %param.9) | copy-start | bytes 172036
  211.4 2.3 copy-start.3
Sparse Core Ops, SparseCore 0:
  213.8 120.0 all-reduce.2
where the time goes:
time: 343 us; the launch traced here: 342 us
  blocking collectives  131 us (38%)
  waiting for transfers between devices  119 us (35%)
  matrix products  50.1 us (15%)
  local copies, waits for them, and re-layouts  19.3 us (6%)
  between operations  14.2 us (4%)
  other arithmetic  8.9 us (3%)
    all_to_all x1, blocking collectives, on_device(): lax.all_to_all(hybrid, 'ro', split_axis=2, concat_axis=3, tiled=True)  131 us
    unnamed x2, waiting for transfers between devices  119 us
    dot_general x1, matrix products, on_device(): jnp.einsum('nk,cakz->canz', ky_sine, hyb_imag, preferred_element_type=jnp...  9.9 us
    dot_general x1, matrix products, on_device(): jnp.einsum('nk,cakz->canz', ky_cosine, hyb_imag, preferred_element_type=j...  8.83 us
    dot_general x1, matrix products, on_device(): jnp.einsum('nk,cakz->canz', ky_sine, hyb_real, preferred_element_type=jnp...  8.54 us
    dot_general x1, matrix products, on_device(): jnp.einsum('nk,cakz->canz', ky_cosine, hyb_real, preferred_element_type=j...  8.53 us
    another operation x2, local copies, waits for them, and re-layouts  7.41 us
  transfers between devices with their start and end apart: 1, of which 1 were waited for; matrix products, arithmetic and copies ran while one was open for 0% of the time, Pallas kernels for 0%

commit v1 on v0

--- a/solution.py
+++ b/solution.py
@@ -1,8 +1,19 @@
+import functools
 import math
 import jax
 import jax.numpy as jnp
 from jax import lax
 from jax.sharding import PartitionSpec as P
+
+
+def get_levels_all(z, named_axis):
+    a_now = lax.axis_size(named_axis)
+    top = jnp.split(z, a_now, 2)
+    local_next = jnp.stack(top, 0)
+    return jnp.concatenate(lax.all_to_all(local_next, named_axis, 0, 0), 3)
+
+
+apply_targets = functools.partial(get_levels_all, named_axis="ro")
 
 
 def dft_tables(length):
@@ -54,7 +65,7 @@
     )
     filtered = (kspace.astype(jnp.float32) * (weight_y * weight_z)).astype(jnp.bfloat16)
     hybrid = kz_transform(filtered, kz_cosine, kz_sine)
-    moved = lax.all_to_all(hybrid, "ro", split_axis=2, concat_axis=3, tiled=True)
+    moved = apply_targets(hybrid)
     hyb_real, hyb_imag = (moved[0], moved[1])
     img_real = jnp.einsum(
         "nk,cakz->canz", ky_cosine, hyb_real, preferred_element_type=jnp.float32

time: 343 us -> 326 us (0.950)
  waiting for transfers between devices: 119 us -> 88.2 us
  other arithmetic: 8.9 us -> 23.3 us
    unnamed x2 -> x1, waiting for transfers between devices: 119 us -> 0.02 us
    reduce_scatter x0 -> x1, waiting for transfers between devices: none -> 88.2 us  [on_device(): lax.psum_scatter(partial_image, 'coil', scatter_dimension=2, tiled=True)]
    another operation x1 -> x4, other arithmetic: 1.1 us -> 14.5 us  [kz_transform(): return jnp.stack([hyb_real, hyb_imag]).astype(jnp.bfloat16)]
    another operation x4, local copies, waits for them, and re-layouts: 12.9 us -> 9.14 us
where the time goes in v1:
time: 326 us; the launch traced here: 325 us
  blocking collectives  131 us (40%)
  waiting for transfers between devices  88.2 us (27%)
  matrix products  50.9 us (16%)
  other arithmetic  23.3 us (7%)
  local copies, waits for them, and re-layouts  17.8 us (5%)
  between operations  14 us (4%)
    all_to_all x1, blocking collectives, get_levels_all(): return jnp.concatenate(lax.all_to_all(local_next, named_axis, 0, 0), 3)  131 us
    reduce_scatter x1, waiting for transfers between devices, on_device(): lax.psum_scatter(partial_image, 'coil', scatter_dimension=2, tiled=True)  88.2 us
    another operation x4, other arithmetic, kz_transform(): return jnp.stack([hyb_real, hyb_imag]).astype(jnp.bfloat16)  14.5 us
    dot_general x1, matrix products, on_device(): jnp.einsum('nk,cakz->canz', ky_sine, hyb_imag, preferred_element_type=jnp...  10.7 us
    dot_general x1, matrix products, on_device(): jnp.einsum('nk,cakz->canz', ky_cosine, hyb_imag, preferred_element_type=j...  8.83 us
    dot_general x1, matrix products, on_device(): jnp.einsum('nk,cakz->canz', ky_sine, hyb_real, preferred_element_type=jnp...  8.54 us
    dot_general x1, matrix products, on_device(): jnp.einsum('nk,cakz->canz', ky_cosine, hyb_real, preferred_element_type=j...  8.54 us
    another operation x2, local copies, waits for them, and re-layouts  7.41 us
  transfers between devices with their start and end apart: 1, of which 1 were waited for; matrix products, arithmetic and copies ran while one was open for 0% of the time, Pallas kernels for 0%

profile of v1, /device:TPU:8, one launch (start us, length us, event | category | flops | bytes accessed | tf_op | source)
XLA Modules:
  0.0 325.1 jit_solution(13415171226506324630)
XLA Ops:
  7.5 0.9 constant_dynamic-slice_fusion
  8.6 0.8 convert_element_type.114
  10.2 2.3 fusion.15
  12.5 3.8 %multiply_convert_fusion = bf16[2,8,32,14,320]{4,2,3,1,0:T(8,128)(2,1)S(1)} fusion(bf16[2,8,32,14,320]{4,2,3,1,0:T(8,128)(2,1)} %param.7, f32[32,14,320]{2,0,1:T(8,128)S(1)} %fusion.15), kind=kLoop, calls=%fused_computation.62 | loop fusion | flops 6881280 | bytes 9748480 | tf_op jit(solution)/shard_map/convert_element_type | solution.py:66
  16.2 3.4 %fusion.6 = f32[8,32,14,320]{3,1,2,0:T(8,128)S(1)} fusion(bf16[2,8,32,14,320]{4,2,3,1,0:T(8,128)(2,1)S(1)} %multiply_convert_fusion), kind=kOutput, calls=%fused_computation.77 | convolution fusion | flops 735129600 | bytes 7340032 | tf_op jit(solution)/shard_map/cakz,zn->cakn/dot_general | solution.py:40
  19.7 3.4 %fusion.7 = f32[8,32,14,320]{3,1,2,0:T(8,128)S(1)} fusion(bf16[2,8,32,14,320]{4,2,3,1,0:T(8,128)(2,1)S(1)} %multiply_convert_fusion), kind=kOutput, calls=%fused_computation.78 | convolution fusion | flops 735129600 | bytes 7340032 | tf_op jit(solution)/shard_map/cakz,zn->cakn/dot_general | solution.py:37
  23.1 3.8 %fusion.5 = bf16[1,8,32,14,320]{4,2,3,1,0:T(8,128)(2,1)S(1)} fusion(f32[8,32,14,320]{3,1,2,0:T(8,128)S(1)} %fusion.6, bf16[2,8,32,14,320]{4,2,3,1,0:T(8,128)(2,1)S(1)} %multiply_convert_fusion), kind=kOutput, calls=%fused_computation.74 | convolution fusion | flops 737423360 | bytes 10551296 | tf_op jit(solution)/shard_map/cakz,zn->cakn/dot_general | solution.py:42
  26.9 3.6 %fusion.4 = bf16[1,8,32,14,320]{4,2,3,1,0:T(8,128)(2,1)S(1)} fusion(f32[8,32,14,320]{3,1,2,0:T(8,128)S(1)} %fusion.7, bf16[2,8,32,14,320]{4,2,3,1,0:T(8,128)(2,1)S(1)} %multiply_convert_fusion), kind=kOutput, calls=%fused_computation.73 | convolution fusion | flops 737423360 | bytes 10551296 | tf_op jit(solution)/shard_map/cakz,zn->cakn/dot_general | solution.py:39
  30.5 2.4 fusion.61
  32.9 4.3 %fusion.62 = (bf16[2,8,1,14,320]{4,2,3,1,0:T(2,128)(2,1)S(1)}, bf16[2,8,1,14,320]{4,2,3,1,0:T(2,128)(2,1)S(1)}, bf16[2,8,1,14,320]{4,2,3,1,0:T(2,128)(2,1)S(1)},...) fusion(bf16[1,8,32,14,320]{4,2,3,1,0:T(8,128)(2,1)S(1)} %fusion, ...), kind=kLoop, calls=%fused_computation.142 | loop fusion | flops 645120 | bytes 5877760 | tf_op jit(solution)/shard_map/stack | solution.py:43
  37.2 3.5 %pad_maximum_fusion.1 = (bf16[2,8,1,14,320]{4,2,3,1,0:T(2,128)(2,1)S(1)}, bf16[2,8,1,14,320]{4,2,3,1,0:T(2,128)(2,1)S(1)}, bf16[2,8,1,14,320]{4,2,3,1,0:T(2,128)...) fusion(bf16[1,8,32,14,320]{4,2,3,1,0:T(8,128)(2,1)S(1)} %fusion, ...), kind=kLoop, calls=%fused_computation.143 | loop fusion | flops 2580480 | bytes 5877760 | tf_op jit(solution)/shard_map/stack | solution.py:43
  40.7 4.3 %fusion.32 = (bf16[2,8,1,14,320]{4,2,3,1,0:T(2,128)(2,1)S(1)}, bf16[2,8,1,14,320]{4,2,3,1,0:T(2,128)(2,1)S(1)}, bf16[2,8,1,14,320]{4,2,3,1,0:T(2,128)(2,1)S(1)},...) fusion(bf16[1,8,32,14,320]{4,2,3,1,0:T(8,128)(2,1)S(1)} %fusion, ...), kind=kLoop, calls=%fused_computation.112 | loop fusion | flops 645120 | bytes 5877760 | tf_op jit(solution)/shard_map/stack | solution.py:43
  47.5 1.7 copy.1977
  49.2 130.9 %all_to_all.5 = bf16[32,2,8,1,14,320]{5,2,4,3,1,0:T(8,128)(2,1)S(1)} all-to-all(bf16[32,2,8,1,14,320]{5,2,4,3,1,0:T(8,128)(2,1)S(1)} %copy.1977), channel_id=1, replica_groups=mesh['coil'=8,'ro'=32] {'ro'}, dimensions={0} | all-to-all | bytes 9175040 | tf_op jit(solution)/shard_map/all_to_all | solution.py:13
  180.1 3.1 fusion.103
  183.2 3.7 %copy.1978 = bf16[8,448,320]{1,2,0:T(8,128)(2,1)S(1)} copy(bf16[8,448,320]{2,0,1:T(8,128)(2,1)} %bitcast.158) | data formatting | bytes 4587520 | tf_op jit(solution)/shard_map/reshape.4
  186.9 8.5 %fusion.26 = f32[8,320,448]{2,1,0:T(8,128)} fusion(bf16[8,448,320]{1,2,0:T(8,128)(2,1)S(1)} %copy.1978), kind=kOutput, calls=%fused_computation.110 | convolution fusion | flops 1029812224 | bytes 6881280 | tf_op jit(solution)/shard_map/nk,cakz->canz/dot_general | solution.py:73
  195.4 8.5 %fusion.30 = f32[8,320,448]{2,1,0:T(8,128)} fusion(bf16[8,448,320]{1,2,0:T(8,128)(2,1)S(1)} %copy.1978), kind=kOutput, calls=%fused_computation.111 | convolution fusion | flops 1029812224 | bytes 6881280 | tf_op jit(solution)/shard_map/nk,cakz->canz/dot_general | solution.py:70
  204.0 3.7 %copy.1979 = bf16[8,448,320]{1,2,0:T(8,128)(2,1)S(1)} copy(bf16[8,448,320]{2,0,1:T(8,128)(2,1)} %bitcast.157) | data formatting | bytes 4587520 | tf_op jit(solution)/shard_map/reshape.8
  207.7 8.8 %convolution_add_fusion = f32[8,320,448]{2,1,0:T(8,128)S(1)} fusion(f32[8,320,448]{2,1,0:T(8,128)} %fusion.26, bf16[8,448,320]{1,2,0:T(8,128)(2,1)S(1)} %copy.1979), kind=kOutput, calls=%fused_computation.79 | convolution fusion | flops 1030959104 | bytes 11468800 | tf_op jit(solution)/shard_map/nk,cakz->canz/dot_general | solution.py:75
  216.6 10.7 %fusion.1 = (f32[448,320]{0,1:T(8,128)}, f32[448,320]{0,1:T(8,128)S(1)}) fusion(f32[8,320,448]{2,1,0:T(8,128)S(1)} %convolution_add_fusion, bf16[2,8,1,448,320]{3,4,2,1,0:T(8,128)(2,1)} %param.8, f32[8,320,448]{2,1,0:T(8,128)S(1)} %copy-done.2, bf16[8,448,320]{1,2,0:T(8,128)(2,1)S(1)} %copy.1979), kind=kOutput, calls=%fused_computation.70 | convolution fusion | flops 1042141184 | bytes 17203200 | tf_op jit(solution)/shard_map/nk,cakz->canz/dot_general | solution.py:72
  227.3 1.3 copy.1982
  228.9 1.2 pad_maximum_fusion
  230.1 88.2 %reduce-scatter.2.cloned.1.call-done = f32[2,1,56,320]{3,2,1,0:T(8,128)} async-done(((f32[2,1,448,320]{3,2,1,0:T(8,128)}), f32[2,1,56,320]{3,2,1,0:T(8,128)}) %reduce-scatter.2.cloned.1.call-update) | async-done | bytes 143376 | tf_op jit(solution)/shard_map/reduce_scatter | solution.py:81
  (82 shorter events, 4.3 us)
Async XLA Ops:
  6.5 0.8 copy-start
  6.5 311.7 %reduce-scatter.2.cloned.1.call-start = ((), (), s32[]{:S(2)}) async-start(), calls=%async_computation.2 | async-start | bytes 1548288 | tf_op jit(solution)/shard_map/reduce_scatter | solution.py:81
  207.7 8.9 %copy-start.2 = (f32[8,320,448]{2,1,0:T(8,128)S(1)}, f32[8,320,448]{2,1,0:T(8,128)}, u32[]{:S(2)}) copy-start(f32[8,320,448]{2,1,0:T(8,128)} %fusion.30) | copy-start | bytes 13762564
  216.5 101.7 %copy-start.1 = (s32[32,448]{1,0:T(8,128)S(1)}, s32[32,448]{1,0:T(8,128)}, u32[]{:S(2)}) copy-start(s32[32,448]{1,0:T(8,128)} %param.9) | copy-start | bytes 172036
Sparse Core Ops, SparseCore 0:
  230.2 87.9 reduce-scatter.1
